TPU v7x, 32 devices: a whole 2x2x4 slice. The times are simulated.
32 devices in a mesh: frow: 4 (over y, x), fcol: 2 (over core), sub: 4 (over z).
Axes of the slice: x: 2, y: 2, z: 4, core: 2. Of those that a mesh axis runs over, the one named last changes fastest.
Arguments:
- contrib: bfloat16 [4, 8192, 4096], P('sub', 'frow', 'fcol'), may hold values from -6 to 6, as said below
- row_map: int32 [4, 16], replicated, may hold values from -1 to 63, as said below
- front_slot: int32 [64], replicated, may hold values from 0 to 63, as said below
- own_diag: float32 [32768], P('frow'), may hold values from 128 to 256
- pattern: int32 [64, 8], P('frow', ('fcol', 'sub')), may hold values 0 or 1
Outputs:
- window: float32 [32768, 4096], P('frow', ('fcol', 'sub'))
Inputs may be any that keep to these rules, and one draw needn't show every extreme that they name: `contrib`: each child's contribution entries. `front_slot`: A permutation of 0 to 63. `row_map`: each child's live rows come first and number 16 - 1 to 16, some child having all 16 live; a child's live entries are distinct; every child has a live row that maps to front block row 0; live row f * 4 + g + m (0 <= m < 1) of a child goes to a front row i with front_slot[i] // 16 = g.
All inputs are finite; a program needn't handle non-finite values. No bound on the sum of `pattern` on one device may be relied on, other than what follows from the above.
Results may differ from a plain program's by a relative error of at most 0.0025.
Values may be sent and summed in bfloat16 or wider, within the bound.
No kernel may reach another device: no remote copies, remote signals or barrier semaphores. Data moves between devices by JAX's collectives and lax.ppermute only.
A program may use at most 192 MiB of HBM per device.

v0:
```python
import jax
import jax.numpy as jnp
from jax import lax
from jax.sharding import PartitionSpec as P

BLK = 512
FB = 64


def from_root(block, axis, source):
    block = jnp.where(lax.axis_index(axis) == source, block, jnp.zeros_like(block))
    return lax.psum(block, axis)


def on_device(contrib, row_map, front_slot, own_diag, pattern):
    owner_count = lax.axis_size("frow")
    child_count = lax.axis_size("sub")
    owner_blocks = FB // owner_count
    row_index = lax.axis_index("frow")
    column = lax.axis_index(("fcol", "sub"))
    local_rows = contrib.shape[1] // BLK
    per_owner = local_rows // owner_count
    pieces = contrib[0].reshape(owner_count, per_owner, BLK, child_count, BLK)
    grouped_map = row_map.reshape(child_count, owner_count, owner_count, per_owner)
    here_map = lax.dynamic_index_in_dim(grouped_map, row_index, 2, keepdims=False)
    here_map = jnp.transpose(here_map, (1, 2, 0))
    live_here = here_map >= 0
    stored_here = front_slot[jnp.maximum(here_map, 0)]
    matches = live_here & (stored_here // owner_blocks == row_index)
    position_here = stored_here - row_index * owner_blocks
    local_slots = jnp.arange(owner_blocks)[:, None, None, None]
    assignment = jnp.where(matches[None] & (position_here[None] == local_slots), 1.0, 0.0).astype(
        jnp.bfloat16
    )
    received = lax.all_to_all(
        lax.all_to_all(pieces, "frow", split_axis=0, concat_axis=0, tiled=True),
        "sub",
        split_axis=3,
        concat_axis=3,
        tiled=True,
    )
    blocks = jnp.einsum("qfmc,fmacb->qab", assignment, received, preferred_element_type=jnp.float32)
    home_slot = front_slot[column]
    owns_home = home_slot // owner_blocks == row_index
    position = jnp.clip(home_slot - row_index * owner_blocks, 0, owner_blocks - 1)
    values = lax.dynamic_index_in_dim(
        own_diag.reshape(owner_blocks, BLK), position, 0, keepdims=False
    )
    diagonal_add = jnp.diag(values) * jnp.where(owns_home, 1.0, 0.0)
    current = lax.dynamic_index_in_dim(blocks, position, 0, keepdims=False)
    assembled = lax.dynamic_update_index_in_dim(blocks, current + diagonal_add, position, 0)
    home_slot = front_slot[0]
    root_row = home_slot // owner_blocks
    position = home_slot % owner_blocks
    diagonal = lax.dynamic_index_in_dim(assembled, position, 0, keepdims=False)
    diagonal = from_root(diagonal.astype(jnp.bfloat16), "frow", root_row).astype(diagonal.dtype)
    symmetric = 0.5 * (diagonal + diagonal.T)
    cholesky_factor = jnp.linalg.cholesky(symmetric)
    identity = jnp.eye(BLK, dtype=jnp.float32)
    inverse = lax.linalg.triangular_solve(cholesky_factor, identity, left_side=True, lower=True)
    panel = jnp.dot(
        assembled.reshape(-1, BLK),
        inverse.T,
        precision=lax.Precision.HIGHEST,
        preferred_element_type=jnp.float32,
    )
    shared = from_root(panel.astype(jnp.bfloat16), ("fcol", "sub"), 0)
    home_slot = front_slot[column]
    root_row = home_slot // owner_blocks
    position = home_slot % owner_blocks
    column_piece = lax.dynamic_index_in_dim(
        shared.reshape(owner_blocks, BLK, BLK), position, 0, keepdims=False
    )
    column_piece = from_root(column_piece, "frow", root_row)
    update = jnp.einsum("ra,ba->rb", shared, column_piece, preferred_element_type=jnp.float32)
    pattern_gate = pattern[:, 0].astype(jnp.float32)
    trailing = (
        assembled - pattern_gate[:, None, None] * update.reshape(owner_blocks, BLK, BLK)
    ).reshape(-1, BLK)
    return jnp.where(column == 0, panel, trailing)


def solution(mesh):
    return jax.shard_map(
        on_device,
        mesh=mesh,
        in_specs=(P("sub", "frow", "fcol"), P(), P(), P("frow"), P("frow", ("fcol", "sub"))),
        out_specs=P("frow", ("fcol", "sub")),
        check_vma=False,
    )
```

profile of v0, /device:TPU:0, one launch (start us, length us, event | category | flops | bytes accessed | tf_op | source)
XLA Modules:
  0.0 899.4 jit_solution(4407061158511109020)
XLA Ops:
  6.5 14.5 %reshape_squeeze.3 = bf16[4,1,512,4,512]{4,3,2,0,1:T(4,128)(2,1)} reshape(bf16[1,2048,2048]{2,1,0:T(8,128)(2,1)} %param.5) | data formatting | bytes 16777216 | tf_op jit(solution)/shard_map/reshape;squeeze | solution.py:23
  21.0 98.5 %all_to_all.10 = bf16[4,1,512,4,512]{4,3,2,1,0:T(4,128)(2,1)S(1)} all-to-all(bf16[4,1,512,4,512]{4,3,2,1,0:T(4,128)(2,1)} %bitcast.96), channel_id=1, replica_groups=mesh['frow'=4,'fcol'=2,'sub'=4] {'frow'}, dimensions={0} | all-to-all | bytes 16777216 | tf_op jit(solution)/shard_map/all_to_all | solution.py:36
  119.5 20.9 %copy.44 = bf16[4,1,512,4,512]{4,0,2,1,3:T(4,128)(2,1)} copy(bf16[4,1,512,4,512]{4,3,2,1,0:T(4,128)(2,1)S(1)} %all_to_all.10) | data formatting | bytes 16777216 | tf_op jit(solution)/shard_map/all_to_all | solution.py:36
  140.4 5.7 all-to-all-start.1
  146.1 0.6 fusion.59
  152.0 0.7 gather_fusion
  153.9 174.5 %all-to-all-done.1 = bf16[4,1,512,4,512]{4,0,2,1,3:T(4,128)(2,1)} async-done(((bf16[4,1,512,4,512]{4,0,2,1,3:T(4,128)(2,1)}), bf16[4,1,512,4,512]{4,0,2,1,3:T(4,128)(2,1)}, u32[]{:S(2)}, u32[]{:S(2)}) %all-to-all-start.1) | async-done | bytes 8388640 | tf_op jit(solution)/shard_map/all_to_all | solution.py:35
  328.4 11.5 %convolution_bitcast_fusion = f32[16,512,512]{2,0,1:T(8,128)} fusion(bf16[4,1,512,4,512]{4,0,2,1,3:T(4,128)(2,1)} %all-to-all-done.1, s32[4,4]{0,1:T(4,128)S(1)} %copy.42, pred[4,4]{0,1:T(4,128)(4,1)S(1)} %fusion.52), kind=kOutput, calls=%fused_computation.5 | convolution fusion | flops 134218752 | bytes 25165904 | tf_op jit(solution)/shard_map/qfmc,fmacb->qab/dot_general | solution.py:42
  339.9 19.3 %copy.47 = f32[16,512,512]{1,2,0:T(8,128)} copy(f32[16,512,512]{2,0,1:T(8,128)} %convolution_bitcast_fusion) | data formatting | bytes 33554432 | tf_op jit(solution)/shard_map/qfmc,fmacb->qab/dot_general | solution.py:42
  359.2 2.4 add_dynamic-update-slice_fusion
  361.5 2.1 fusion.18
  363.9 17.8 %copy.48 = f32[16,512,512]{2,1,0:T(8,128)} copy(f32[16,512,512]{1,2,0:T(8,128)} %add_dynamic-update-slice_fusion) | data formatting | bytes 33554432 | tf_op jit(solution)/shard_map/jit(dynamic_update_index_in_dim)/dynamic_update_slice | solution.py:51
  381.7 25.4 %all-reduce.5.cloned.1.call-done = bf16[512,512]{0,1:T(8,128)(2,1)} async-done(((bf16[512,512]{0,1:T(8,128)(2,1)}), bf16[512,512]{0,1:T(8,128)(2,1)}) %all-reduce.5.cloned.1.call-update) | async-done | bytes 524304 | tf_op jit(solution)/shard_map/psum | solution.py:12
  407.1 1.3 copy.49
  408.4 1.2 fusion.11
  410.1 1.0 copy-done.1
  411.1 11.7 %cholesky.103 = f32[128,128]{1,0:T(8,128)S(1)} custom-call(f32[128,128]{1,0:T(8,128)S(1)} %cholesky.263), custom_call_target="Cholesky" | custom-call | tf_op jit(solution)/shard_map/jit(cholesky)/cholesky | solution.py:58
  423.0 9.8 %custom-call.30 = f32[1,128,128]{1,2,0:T(8,128)S(1)} custom-call(f32[1,128,128]{2,1,0:T(8,128)S(1)} %get-tuple-element.32), custom_call_target="InvertDiagBlocksLowerTriangular" | custom-call | tf_op jit(solution)/shard_map/jit(cholesky)/cholesky | solution.py:58
  432.8 1.2 constant_dynamic-update-slice_fusion
  434.1 1.3 convolution_subtract_fusion.3
  435.4 11.7 %cholesky.215 = f32[128,128]{1,0:T(8,128)S(1)} custom-call(f32[128,128]{1,0:T(8,128)S(1)} %cholesky.267), custom_call_target="Cholesky" | custom-call | tf_op jit(solution)/shard_map/jit(cholesky)/cholesky | solution.py:58
  447.1 10.0 %custom-call.31 = f32[1,128,128]{1,2,0:T(8,128)S(1)} custom-call(f32[1,128,128]{2,1,0:T(8,128)S(1)} %get-tuple-element.29), custom_call_target="InvertDiagBlocksLowerTriangular" | custom-call | tf_op jit(solution)/shard_map/jit(cholesky)/cholesky | solution.py:58
  457.4 1.3 convolution_subtract_fusion.4
  458.7 11.7 %cholesky.236 = f32[128,128]{1,0:T(8,128)S(1)} custom-call(f32[128,128]{1,0:T(8,128)S(1)} %cholesky.272), custom_call_target="Cholesky" | custom-call | tf_op jit(solution)/shard_map/jit(cholesky)/cholesky | solution.py:58
  470.4 9.8 %custom-call.32 = f32[1,128,128]{1,2,0:T(8,128)S(1)} custom-call(f32[1,128,128]{2,1,0:T(8,128)S(1)} %get-tuple-element.26), custom_call_target="InvertDiagBlocksLowerTriangular" | custom-call | tf_op jit(solution)/shard_map/jit(cholesky)/cholesky | solution.py:58
  480.4 1.2 convolution_subtract_fusion.5
  481.7 12.1 %cholesky.253 = f32[128,128]{1,0:T(8,128)S(1)} custom-call(f32[128,128]{1,0:T(8,128)S(1)} %convolution_subtract_fusion.5), custom_call_target="Cholesky" | custom-call | tf_op jit(solution)/shard_map/jit(cholesky)/cholesky | solution.py:58
  493.8 0.7 compare_reduce_fusion.2
  494.5 0.6 compare_reduce_fusion.1
  495.1 0.7 compare_reduce_fusion.3
  498.5 10.5 %while.1 = (s32[]{:T(128)}, f32[512,512]{1,0:T(8,128)S(1)}, s32[4,2]{0,1:T(2,128)S(1)}, f32[4,128,128]{2,1,0:T(8,128)}, s32[]{:T(128)}) while((s32[]{:T(128)}, f32[512,512]{1,0:T(8,128)S(1)}, s32[4,2]{0,1:T(2,128)S(1)}, f32[4,128,128]{2,1,0:T(8,128)}, s32[]{:T(128)}) %tuple.29), condition=%wide.while_cond, body=%wide.while_body.sunk | while | flops 2 | bytes 132205 | solution.py:60
  498.6 0.6 fusion.70
  499.2 2.0 bitcast_dynamic-update-slice_fusion.2
  501.8 2.0 bitcast_dynamic-update-slice_fusion.2
  504.5 2.0 bitcast_dynamic-update-slice_fusion.2
  507.1 2.0 bitcast_dynamic-update-slice_fusion.2
  509.1 40.1 %custom-call.33 = f32[4,128,128]{1,2,0:T(8,128)S(1)} custom-call(f32[4,128,128]{2,1,0:T(8,128)} %get-tuple-element.12), custom_call_target="InvertDiagBlocksLowerTriangular" | custom-call | tf_op jit(solution)/shard_map/triangular_solve | solution.py:60
  551.2 0.6 convolution_subtract_fusion.2
  552.3 31.9 %convert_select_fusion = (bf16[8192,512]{1,0:T(8,128)(2,1)}, f32[8192,512]{1,0:T(8,128)}) fusion(pred[]{:T(512)S(6)} %eq.66, f32[8192,512]{1,0:T(8,128)} %bitcast.94, f32[128,512]{1,0:T(8,128)S(1)} %fusion.33, f32[128,512]{1,0:T(8,128)S(1)} %fusion.34, f32[128,512]{1,0:T(8,128)S(1)} %fusion.36, f32[128,512]{1,0:T(8,128)S(1)} %fusion.24), kind=kOutput, calls=%fused_computation.8 | convolution fusion | flops 25778978816 | bytes 42991616 | tf_op jit(solution)/shard_map/dot_general | solution.py:61
  584.4 175.4 %all-reduce.7.cloned.1.call-done = bf16[8192,512]{1,0:T(8,128)(2,1)} async-done(((bf16[8192,512]{1,0:T(8,128)(2,1)}), bf16[8192,512]{1,0:T(8,128)(2,1)}) %all-reduce.7.cloned.1.call-update) | async-done | bytes 8388624 | tf_op jit(solution)/shard_map/psum | solution.py:12
  759.9 1.1 constant_dynamic-slice_fusion.1
  761.2 0.8 select_bitcast_fusion
  762.0 46.3 %all-reduce.9.cloned.1.call-done = bf16[512,512]{0,1:T(8,128)(2,1)} async-done(((bf16[512,512]{0,1:T(8,128)(2,1)}), bf16[512,512]{0,1:T(8,128)(2,1)}) %all-reduce.9.cloned.1.call-update) | async-done | bytes 524304 | tf_op jit(solution)/shard_map/psum | solution.py:12
  808.4 14.1 %fusion.60 = f32[8192,512]{1,0:T(8,128)} fusion(bf16[8192,512]{1,0:T(8,128)(2,1)} %all-reduce.7.cloned.1.call-done, bf16[512,512]{0,1:T(8,128)(2,1)} %all-reduce.9.cloned.1.call-done), kind=kOutput, calls=%fused_computation.120 | convolution fusion | flops 4294967296 | bytes 25690112 | tf_op jit(solution)/shard_map/ra,ba->rb/dot_general | solution.py:75
  822.5 17.6 %copy.52 = f32[16,512,512]{1,2,0:T(8,128)} copy(f32[16,512,512]{2,1,0:T(8,128)} %bitcast.95) | data formatting | bytes 33554432 | tf_op jit(solution)/shard_map/reshape | solution.py:78
  840.1 17.4 %multiply_subtract_fusion = f32[16,512,512]{1,2,0:T(8,128)} fusion(f32[16,512,512]{1,2,0:T(8,128)} %add_dynamic-update-slice_fusion, f32[16,512,512]{1,2,0:T(8,128)} %copy.52, f32[16]{0:T(128)S(1)} %convert_bitcast_fusion), kind=kLoop, calls=%fused_computation.4 | loop fusion | flops 8388608 | bytes 50331712 | tf_op jit(solution)/shard_map/sub | solution.py:78
  857.5 17.6 %copy.53 = f32[16,512,512]{2,1,0:T(8,128)} copy(f32[16,512,512]{1,2,0:T(8,128)} %multiply_subtract_fusion) | data formatting | bytes 33554432 | tf_op jit(solution)/shard_map/sub | solution.py:78
  875.1 17.6 %bitcast_select_fusion = f32[8192,512]{1,0:T(8,128)} fusion(f32[8192,512]{1,0:T(8,128)} %get-tuple-element.38, f32[16,512,512]{2,1,0:T(8,128)} %copy.53, pred[]{:T(512)S(6)} %eq.66), kind=kLoop, calls=%fused_computation.3 | loop fusion | flops 4194304 | bytes 50331648 | tf_op jit(solution)/shard_map/jit(_where)/select_n | solution.py:80
  (61 shorter events, 7.7 us)
Async XLA Ops:
  119.5 26.6 %copy-start = (s32[64]{0:T(128)S(1)}, s32[64]{0:T(128)}, u32[]{:S(2)}) copy-start(s32[64]{0:T(128)} %param.7) | copy-start | bytes 772
  119.5 32.0 %copy-start.3 = (s32[4,16]{1,0:T(4,128)S(1)}, s32[4,16]{1,0:T(4,128)}, u32[]{:S(2)}) copy-start(s32[4,16]{1,0:T(4,128)} %param.6) | copy-start | bytes 772
  119.5 34.1 %copy-start.2 = (f32[8192]{0:T(1024)S(1)}, f32[8192]{0:T(1024)}, u32[]{:S(2)}) copy-start(f32[8192]{0:T(1024)} %param.8) | copy-start | bytes 98308
  140.4 188.0 %all-to-all-start.1 = ((bf16[4,1,512,4,512]{4,0,2,1,3:T(4,128)(2,1)}), bf16[4,1,512,4,512]{4,0,2,1,3:T(4,128)(2,1)}, u32[]{:S(2)}, u32[]{:S(2)}) async-start(bf16[4,1,512,4,512]{4,0,2,1,3:T(4,128)(2,1)} %copy.44), calls=%async_computation.1 | async-start | bytes 16777216 | tf_op jit(solution)/shard_map/all_to_all | solution.py:35
  146.0 261.1 %all-reduce.5.cloned.1.call-start = ((), (), s32[]{:S(2)}) async-start(), calls=%async_computation.2 | async-start | bytes 1048576 | tf_op jit(solution)/shard_map/psum | solution.py:12
  363.6 396.2 %all-reduce.7.cloned.1.call-start = ((), (), s32[]{:S(2)}) async-start(), calls=%async_computation.3 | async-start | bytes 16777216 | tf_op jit(solution)/shard_map/psum | solution.py:12
  410.1 1.0 copy-start.1
  552.3 209.8 %copy-start.4 = (s32[16,1]{0,1:T(1,128)S(1)}, s32[16,1]{0,1:T(1,128)}, u32[]{:S(2)}) copy-start(s32[16,1]{0,1:T(1,128)} %param.9) | copy-start | bytes 196
  584.2 224.2 %all-reduce.9.cloned.1.call-start = ((), (), s32[]{:S(2)}) async-start(), calls=%async_computation.4 | async-start | bytes 1048576 | tf_op jit(solution)/shard_map/psum | solution.py:12
Sparse Core Ops, SparseCore 0:
  363.8 43.2 all-reduce.4
  584.3 175.5 all-reduce.6
  762.9 45.4 all-reduce.8
where the time goes:
time: 907 us; the launch traced here: 899 us
  waiting for transfers between devices  422 us (47%)
  other arithmetic  162 us (18%)
  local copies, waits for them, and re-layouts  124 us (14%)
  blocking collectives  98.5 us (11%)
  matrix products  66 us (7%)
  between operations  21.7 us (2%)
    psum x3, waiting for transfers between devices, from_root(): return lax.psum(block, axis)  247 us
    all_to_all x1, waiting for transfers between devices, on_device(): lax.all_to_all(lax.all_to_all(pieces, 'frow', split_axis=0, concat_axis=0...  174 us
    all_to_all x1, blocking collectives, on_device(): lax.all_to_all(pieces, 'frow', split_axis=0, concat_axis=0, tiled=True)  98.5 us
    another operation x14, other arithmetic, on_device(): cholesky_factor = jnp.linalg.cholesky(symmetric)  79 us
    another operation x3, other arithmetic, on_device(): lax.linalg.triangular_solve(cholesky_factor, identity, left_side=True, lo...  40.3 us
    dot_general x1, matrix products, on_device(): jnp.dot(assembled.reshape(-1, BLK), inverse.T, precision=lax.Precision.HI...  31.9 us
    all_to_all x1, local copies, waits for them, and re-layouts, on_device(): lax.all_to_all(pieces, 'frow', split_axis=0, concat_axis=0, tiled=True)  20.9 us
    dot_general x1, local copies, waits for them, and re-layouts, on_device(): jnp.einsum('qfmc,fmacb->qab', assignment, received, preferred_element_typ...  19.3 us
  transfers between devices with their start and end apart: 4, of which 4 were waited for; matrix products, arithmetic and copies ran while one was open for 2% of the time, Pallas kernels for 0%

commit v1 on v0

--- a/solution.py
+++ b/solution.py
@@ -7,9 +7,13 @@
 FB = 64
 
 
+def unite_tokens_on(content, net_axis):
+    return jax.lax.all_gather(content, axis_name=net_axis).sum(axis=0)
+
+
 def from_root(block, axis, source):
     block = jnp.where(lax.axis_index(axis) == source, block, jnp.zeros_like(block))
-    return lax.psum(block, axis)
+    return unite_tokens_on(block, net_axis=axis)
 
 
 def on_device(contrib, row_map, front_slot, own_diag, pattern):

time: 907 us -> 1290 us (1.42)
  waiting for transfers between devices: 422 us -> 786 us
  other arithmetic: 162 us -> 176 us
    all_gather x0 -> x3, waiting for transfers between devices: none -> 612 us  [unite_tokens_on(): return jax.lax.all_gather(content, axis_name=net_axis).sum(axis=0)]
    psum x3 -> x0, waiting for transfers between devices: 247 us -> none  [from_root(): return lax.psum(block, axis)]
    reduce_sum x0 -> x3, other arithmetic: none -> 30.2 us  [unite_tokens_on(): return jax.lax.all_gather(content, axis_name=net_axis).sum(axis=0)]
    dynamic_update_slice x1 -> x2, local copies, waits for them, and re-layouts: 17.8 us -> 39.4 us  [on_device(): lax.dynamic_update_index_in_dim(blocks, current + diagonal_add, position, 0)]
    reshape x1 -> x0, local copies, waits for them, and re-layouts: 17.6 us -> none  [on_device(): update.reshape(owner_blocks, BLK, BLK)]
    sub x1 -> x0, other arithmetic: 17.4 us -> none  [on_device(): assembled - pattern_gate[:, None, None] * update.reshape(owner_blocks, BL...]
where the time goes in v1:
time: 1290 us; the launch traced here: 1280 us
  waiting for transfers between devices  786 us (61%)
  other arithmetic  176 us (14%)
  local copies, waits for them, and re-layouts  118 us (9%)
  blocking collectives  98.5 us (8%)
  matrix products  74.2 us (6%)
  between operations  21.6 us (2%)
    all_gather x3, waiting for transfers between devices, unite_tokens_on(): return jax.lax.all_gather(content, axis_name=net_axis).sum(axis=0)  612 us
    all_to_all x1, waiting for transfers between devices, on_device(): lax.all_to_all(lax.all_to_all(pieces, 'frow', split_axis=0, concat_axis=0...  174 us
    all_to_all x1, blocking collectives, on_device(): lax.all_to_all(pieces, 'frow', split_axis=0, concat_axis=0, tiled=True)  98.5 us
    another operation x14, other arithmetic, on_device(): cholesky_factor = jnp.linalg.cholesky(symmetric)  78.7 us
    another operation x3, other arithmetic, on_device(): lax.linalg.triangular_solve(cholesky_factor, identity, left_side=True, lo...  40.4 us
    dynamic_update_slice x2, local copies, waits for them, and re-layouts, on_device(): lax.dynamic_update_index_in_dim(blocks, current + diagonal_add, position, 0)  39.4 us
    dot_general x1, matrix products, on_device(): jnp.dot(assembled.reshape(-1, BLK), inverse.T, precision=lax.Precision.HI...  31.9 us
    reduce_sum x3, other arithmetic, unite_tokens_on(): return jax.lax.all_gather(content, axis_name=net_axis).sum(axis=0)  30.2 us
  transfers between devices with their start and end apart: 4, of which 4 were waited for; matrix products, arithmetic and copies ran while one was open for 2% of the time, Pallas kernels for 0%

profile of v1, /device:TPU:0, one launch (start us, length us, event | category | flops | bytes accessed | tf_op | source)
XLA Modules:
  0.0 1281.3 jit_solution(18398562320239206646)
XLA Ops:
  6.5 14.5 %reshape_squeeze.3 = bf16[4,1,512,4,512]{4,3,2,0,1:T(4,128)(2,1)} reshape(bf16[1,2048,2048]{2,1,0:T(8,128)(2,1)} %param.5) | data formatting | bytes 16777216 | tf_op jit(solution)/shard_map/reshape;squeeze | solution.py:27
  21.0 98.5 %all_to_all.10 = bf16[4,1,512,4,512]{4,3,2,1,0:T(4,128)(2,1)S(1)} all-to-all(bf16[4,1,512,4,512]{4,3,2,1,0:T(4,128)(2,1)} %bitcast.92), channel_id=1, replica_groups=mesh['frow'=4,'fcol'=2,'sub'=4] {'frow'}, dimensions={0} | all-to-all | bytes 16777216 | tf_op jit(solution)/shard_map/all_to_all | solution.py:40
  119.5 20.9 %copy.40 = bf16[4,1,512,4,512]{4,0,2,1,3:T(4,128)(2,1)} copy(bf16[4,1,512,4,512]{4,3,2,1,0:T(4,128)(2,1)S(1)} %all_to_all.10) | data formatting | bytes 16777216 | tf_op jit(solution)/shard_map/all_to_all | solution.py:40
  140.3 5.8 all-to-all-start.1
  152.8 0.7 gather_fusion
  154.0 174.5 %all-to-all-done.1 = bf16[4,1,512,4,512]{4,0,2,1,3:T(4,128)(2,1)} async-done(((bf16[4,1,512,4,512]{4,0,2,1,3:T(4,128)(2,1)}), bf16[4,1,512,4,512]{4,0,2,1,3:T(4,128)(2,1)}, u32[]{:S(2)}, u32[]{:S(2)}) %all-to-all-start.1) | async-done | bytes 8388640 | tf_op jit(solution)/shard_map/all_to_all | solution.py:39
  328.5 11.5 convolution_bitcast_fusion
  340.0 4.5 fusion.3
  344.5 21.7 %dynamic_update_slice.4 = f32[16,512,512]{2,0,1:T(8,128)} dynamic-update-slice(f32[16,512,512]{2,0,1:T(8,128)} %convolution_bitcast_fusion, f32[1,512,512]{2,0,1:T(1,128)S(1)} %fusion.3, s32[]{:T(128)S(6)} %min.4, s32[]{:T(128)} %constant.231.clone.1, s32[]{:T(128)} %constant.231.clone.1) | dynamic-update-slice | bytes 2097156 | tf_op jit(solution)/shard_map/jit(dynamic_update_index_in_dim)/dynamic_update_slice | solution.py:55
  366.2 4.5 broadcast_select_fusion.1
  370.7 0.9 copy.43
  372.4 17.7 %copy.42 = f32[16,512,512]{2,1,0:T(8,128)} copy(f32[16,512,512]{2,0,1:T(8,128)} %dynamic_update_slice.4) | data formatting | bytes 33554432 | tf_op jit(solution)/shard_map/jit(dynamic_update_index_in_dim)/dynamic_update_slice | solution.py:55
  390.1 14.8 %all-gather.5.cloned.1.call-done = bf16[4,512,512]{2,1,0:T(8,128)(2,1)} async-done(((bf16[1,512,512]{2,1,0:T(8,128)(2,1)}), bf16[4,512,512]{2,1,0:T(8,128)(2,1)}) %all-gather.5.cloned.1.call-update) | async-done | bytes 2097168 | tf_op jit(solution)/shard_map/all_gather | solution.py:11
  404.9 2.2 reduce_sum.36
  407.7 1.0 copy-done.1
  408.7 11.7 cholesky.103
  420.6 9.8 custom-call.30
  430.4 1.2 constant_dynamic-update-slice_fusion
  431.7 1.3 convolution_subtract_fusion.3
  432.9 11.7 cholesky.215
  444.7 10.0 custom-call.31
  454.9 1.3 convolution_subtract_fusion.4
  456.2 11.7 cholesky.236
  468.6 9.8 custom-call.32
  478.6 1.2 convolution_subtract_fusion.5
  479.9 11.9 cholesky.253
  492.4 0.7 compare_reduce_fusion.3
  495.6 1.1 select_select_fusion
  496.7 11.7 while.1
  497.4 2.2 bitcast_dynamic-update-slice_fusion.2
  500.3 2.2 bitcast_dynamic-update-slice_fusion.2
  503.2 2.2 bitcast_dynamic-update-slice_fusion.2
  506.2 2.2 bitcast_dynamic-update-slice_fusion.2
  508.4 39.3 %custom-call.33 = f32[4,128,128]{1,2,0:T(8,128)S(1)} custom-call(f32[4,128,128]{2,1,0:T(8,128)S(1)} %get-tuple-element.12), custom_call_target="InvertDiagBlocksLowerTriangular" | custom-call | tf_op jit(solution)/shard_map/triangular_solve | solution.py:64
  548.0 1.2 convolution_subtract_fusion.1
  549.7 1.3 convolution_subtract_fusion
  551.4 1.6 convolution_subtract_fusion.2
  553.4 31.9 %convert_select_fusion = (bf16[8192,512]{1,0:T(8,128)(2,1)}, f32[8192,512]{1,0:T(8,128)}) fusion(pred[]{:T(512)S(6)} %eq.66, f32[8192,512]{1,0:T(8,128)} %bitcast.89, f32[128,512]{1,0:T(8,128)S(1)} %fusion.34, f32[128,512]{1,0:T(8,128)S(1)} %fusion.35, f32[128,512]{1,0:T(8,128)S(1)} %fusion.37, f32[128,512]{1,0:T(8,128)S(1)} %fusion.25), kind=kOutput, calls=%fused_computation.8 | convolution fusion | flops 25778978816 | bytes 42991616 | tf_op jit(solution)/shard_map/dot_general | solution.py:65
  585.8 563.6 %all-gather.9.cloned.1.call-done = bf16[65536,512]{1,0:T(8,128)(2,1)} async-done(((bf16[8192,512]{1,0:T(8,128)(2,1)}), bf16[65536,512]{1,0:T(8,128)(2,1)}) %all-gather.9.cloned.1.call-update) | async-done | bytes 67108880 | tf_op jit(solution)/shard_map/all_gather | solution.py:11
  1149.5 25.8 %reduce_sum.37 = bf16[8192,512]{1,0:T(8,128)(2,1)} reduce(bf16[8,8192,512]{2,1,0:T(8,128)(2,1)} %bitcast.25, bf16[]{:T(256)} %constant.239.clone.1), dimensions={0}, to_apply=%region_9.10 | reduce | flops 29360128 | bytes 75497472 | tf_op jit(solution)/shard_map/reduce_sum | solution.py:11
  1175.3 11.4 copy.47
  1186.6 3.5 broadcast_select_fusion
  1190.2 0.9 copy.48
  1191.1 33.5 %all-gather.7.cloned.1.call-done = bf16[4,512,512]{2,1,0:T(8,128)(2,1)} async-done(((bf16[1,512,512]{2,1,0:T(8,128)(2,1)}), bf16[4,512,512]{2,1,0:T(8,128)(2,1)}) %all-gather.7.cloned.1.call-update) | async-done | bytes 2097168 | tf_op jit(solution)/shard_map/all_gather | solution.py:11
  1224.6 2.2 reduce_sum.38
  1226.8 19.7 %multiply_subtract_fusion = f32[16,512,512]{2,0,1:T(8,128)} fusion(f32[16,512,512]{2,0,1:T(8,128)} %dynamic_update_slice.4, f32[16]{0:T(128)S(1)} %convert_bitcast_fusion, bf16[512,512]{1,0:T(8,128)(2,1)S(1)} %reduce_sum.38, bf16[16,512,512]{2,1,0:T(8,128)(2,1)} %bitcast.91), kind=kOutput, calls=%fused_computation.4 | convolution fusion | flops 4303355904 | bytes 42467392 | tf_op jit(solution)/shard_map/ra,ba->rb/dot_general | solution.py:79
  1246.5 15.2 %copy.50 = f32[16,512,512]{2,1,0:T(8,128)S(1)} copy(f32[16,512,512]{2,0,1:T(8,128)} %multiply_subtract_fusion) | data formatting | bytes 33554432 | tf_op jit(solution)/shard_map/sub | solution.py:82
  1261.7 12.8 %bitcast_select_fusion = f32[8192,512]{1,0:T(8,128)} fusion(f32[8192,512]{1,0:T(8,128)} %get-tuple-element.38, f32[16,512,512]{2,1,0:T(8,128)S(1)} %copy.50, pred[]{:T(512)S(6)} %eq.66), kind=kLoop, calls=%fused_computation.3 | loop fusion | flops 4194304 | bytes 50331648 | tf_op jit(solution)/shard_map/jit(_where)/select_n | solution.py:84
  (62 shorter events, 9.8 us)
Async XLA Ops:
  140.3 5.9 copy-start
  140.3 11.9 copy-start.3
  140.3 13.4 %copy-start.2 = (f32[8192]{0:T(1024)S(1)}, f32[8192]{0:T(1024)}, u32[]{:S(2)}) copy-start(f32[8192]{0:T(1024)} %param.8) | copy-start | bytes 98308
  140.3 188.2 %all-to-all-start.1 = ((bf16[4,1,512,4,512]{4,0,2,1,3:T(4,128)(2,1)}), bf16[4,1,512,4,512]{4,0,2,1,3:T(4,128)(2,1)}, u32[]{:S(2)}, u32[]{:S(2)}) async-start(bf16[4,1,512,4,512]{4,0,2,1,3:T(4,128)(2,1)} %copy.40), calls=%async_computation.1 | async-start | bytes 16777216 | tf_op jit(solution)/shard_map/all_to_all | solution.py:39
  146.1 258.8 %all-gather.5.cloned.1.call-start = ((), (), s32[]{:S(2)}) async-start(), calls=%async_computation.2 | async-start | bytes 2621440 | tf_op jit(solution)/shard_map/all_gather | solution.py:11
  371.6 777.8 %all-gather.9.cloned.1.call-start = ((), (), s32[]{:S(2)}) async-start(), calls=%async_computation.4 | async-start | bytes 75497472 | tf_op jit(solution)/shard_map/all_gather | solution.py:11
  407.7 1.0 copy-start.1
  585.3 639.3 %all-gather.7.cloned.1.call-start = ((), (), s32[]{:S(2)}) async-start(), calls=%async_computation.3 | async-start | bytes 2621440 | tf_op jit(solution)/shard_map/all_gather | solution.py:11
  1175.3 15.8 %copy-start.4 = (s32[16,1]{0,1:T(1,128)S(1)}, s32[16,1]{0,1:T(1,128)}, u32[]{:S(2)}) copy-start(s32[16,1]{0,1:T(1,128)} %param.9) | copy-start | bytes 196
Sparse Core Ops, SparseCore 0:
  371.8 33.0 all-gather.4
  585.5 563.9 all-gather.8
  1191.2 33.3 all-gather.6
